TPU v7x, 256 devices: a whole 4x4x8 slice. The times are simulated.
256 devices in a mesh: seq: 64 (over x_hi, z, y), tp: 4 (over x_lo, core).
Axes of the slice: x: 4 (x_hi: 2, x_lo: 2; x = x_hi * 2 + x_lo), y: 4, z: 8, core: 2. Of those that a mesh axis runs over, the one named last changes fastest.
Arguments:
- query_rows: bfloat16 [16384, 4096], P('seq', 'tp'), may hold values from -130 to 130
- key_rows: bfloat16 [16384, 4096], P('seq', 'tp'), may hold values from -8 to 8
- value_rows: bfloat16 [16384, 4096], P('seq', 'tp'), may hold values from -6 to 6
- cotangent: bfloat16 [16384, 4096], P('seq', 'tp'), may hold values from -6 to 6
- global_pos: int32 [256], P('seq'), may hold values from 0 to 16383, as said below
- partner_mask: int32 [1], replicated, may hold values from 1 to 63
- rand_block: int32 [1, 64], replicated, may hold values from 0 to 1
Outputs:
- attention: bfloat16 [16384, 4096], P('seq', 'tp')
- grad_queries: bfloat16 [16384, 4096], P('seq', 'tp')
- grad_keys: bfloat16 [16384, 4096], P('seq', 'tp')
- grad_values: bfloat16 [16384, 4096], P('seq', 'tp')
Inputs may be any that keep to these rules, and one draw needn't show every extreme that they name: `global_pos`: the tokens of run d (positions d * 256 onward) hold exactly 4 global positions; all are distinct and in increasing order.
All inputs are finite; a program needn't handle non-finite values.
Results may differ from a plain program's by a relative error of at most 0.011.
Values may be sent and summed in bfloat16 or wider, within the bound.
A program may use at most 128 MiB of HBM per device.

v0:
```python
import jax
import jax.numpy as jnp
from jax import lax
from jax.sharding import PartitionSpec as P

HEAD_DIM = 128
BLK = 128


def from_partner(shard, axis, bit):
    return lax.ppermute(shard, axis, [(i, i ^ 1 << bit) for i in range(lax.axis_size(axis))])


def with_halo(shard, sides, width):
    for axis, dim in sides:
        size, length = (lax.axis_size(axis), shard.shape[dim])
        up = [(i, (i + 1) % size) for i in range(size - 1)]
        down = [(j, i) for i, j in up]
        last = lax.slice_in_dim(shard, length - width, length, axis=dim)
        first = lax.slice_in_dim(shard, 0, width, axis=dim)
        before = lax.ppermute(last, axis, up)
        after = lax.ppermute(first, axis, down)
        shard = jnp.concatenate([before, shard, after], axis=dim)
    return shard


def joined(value, axis, join):
    pieces = jax.tree.map(lambda part: lax.all_gather(part, axis), value)
    head = jax.tree.map(lambda part: part[0], pieces)
    tail = jax.tree.map(lambda part: part[1:], pieces)
    total, _ = lax.scan(lambda total, piece: (join(total, piece), None), head, tail)
    return total


def passed_along(block, axis, distance):
    devices = range(lax.axis_size(axis))
    route = [(i - distance, i) for i in devices if i - distance in devices]
    return lax.ppermute(block, axis, route)


def attend(query_inputs, gathered_keys, gathered_values, usable, incoming_gradient):
    softmax_scale_factor = query_inputs.shape[-1] ** (-0.5)
    logit_scores = (
        jnp.einsum("crj,prj->rcp", query_inputs, gathered_keys, preferred_element_type=jnp.float32)
        * softmax_scale_factor
    )
    logit_scores = jnp.where(usable[None, None, :], logit_scores, -1e30)
    maxima = jnp.max(logit_scores, axis=2, keepdims=True)
    raised = jnp.exp(logit_scores - maxima)
    totals = jnp.sum(raised, axis=2, keepdims=True)
    chances = raised / totals
    attention_weight_rows = chances.astype(jnp.bfloat16)
    attention_output = jnp.einsum(
        "bxl,lby->xby", attention_weight_rows, gathered_values, preferred_element_type=jnp.float32
    ).astype(jnp.bfloat16)
    deltas = jnp.transpose(
        jnp.sum(
            incoming_gradient.astype(jnp.float32) * attention_output.astype(jnp.float32), axis=2
        )
    )[:, :, None]
    probability_gradient = jnp.einsum(
        "crj,prj->rcp", incoming_gradient, gathered_values, preferred_element_type=jnp.float32
    )
    scaled_scores = (chances * (probability_gradient - deltas) * softmax_scale_factor).astype(
        jnp.bfloat16
    )
    query_gradient_rows = jnp.einsum(
        "bxl,lby->xby", scaled_scores, gathered_keys, preferred_element_type=jnp.float32
    )
    key_gradient_rows = jnp.einsum(
        "cgi,gcx->icx", scaled_scores, query_inputs, preferred_element_type=jnp.float32
    )
    value_gradient_rows = jnp.einsum(
        "cgi,gcx->icx", attention_weight_rows, incoming_gradient, preferred_element_type=jnp.float32
    )
    return (attention_output, query_gradient_rows, key_gradient_rows, value_gradient_rows)


def merge_stats(first, second):
    maxima = jnp.maximum(first[0], second[0])
    totals = first[1] * jnp.exp(first[0] - maxima) + second[1] * jnp.exp(second[0] - maxima)
    return (maxima, totals)


def level_order(levels):
    return list(range(levels))


def send_blocks(parcel, partner_mask, levels):
    for bit_level in level_order(levels):
        swapped = from_partner(parcel, "seq", bit_level)
        selected = jnp.right_shift(partner_mask, bit_level) % 2 == 1
        parcel = jnp.where(selected[:, None, None], swapped, parcel)
    return parcel


def return_grads(parcel, partner_mask, levels):
    for bit_level in level_order(levels):
        swapped = from_partner(parcel.astype(jnp.bfloat16), "seq", bit_level).astype(parcel.dtype)
        selected = jnp.right_shift(partner_mask, bit_level) % 2 == 1
        parcel = jnp.where(selected[:, None, None], swapped, parcel)
    return parcel


def per_device(query_rows, key_rows, value_rows, cotangent, global_pos, partner_mask, rand_block):
    local_count, columns = query_rows.shape
    head_here = columns // HEAD_DIM
    block_here = local_count // BLK
    rounds_count = partner_mask.shape[0]
    global_here = global_pos.shape[0]
    shard_index = lax.axis_index("seq")
    shard_count = lax.axis_size("seq")
    levels = shard_count.bit_length() - 1
    local_pos = global_pos - shard_index * local_count
    global_query, global_key, global_value, global_cot = (
        lax.all_gather(query_rows[local_pos], "seq", axis=0, tiled=True),
        lax.all_gather(key_rows[local_pos], "seq", axis=0, tiled=True),
        lax.all_gather(value_rows[local_pos], "seq", axis=0, tiled=True),
        lax.all_gather(cotangent[local_pos], "seq", axis=0, tiled=True),
    )
    global_count = global_query.shape[0]
    key_value = jnp.concatenate([key_rows, value_rows], axis=1)
    extended = with_halo(key_value, (("seq", 0),), BLK)
    requester = jnp.bitwise_xor(shard_index, partner_mask)
    chosen = rand_block[jnp.arange(rounds_count, dtype=jnp.int32), requester]
    outgoing = jnp.stack([lax.dynamic_slice_in_dim(key_value, chosen[0] * BLK, BLK, 0)])
    incoming = send_blocks(outgoing, partner_mask, levels)
    random_rows = incoming.reshape(rounds_count * BLK, 2 * columns)
    shared_keys = jnp.concatenate([random_rows[:, :columns], global_key], axis=0)
    shared_values = jnp.concatenate([random_rows[:, columns:], global_value], axis=0)
    shared_count = shared_keys.shape[0]
    global_marks = jnp.any(
        jnp.arange(local_count, dtype=jnp.int32)[:, None] == local_pos[None, :], axis=1
    )
    sparse_cot = jnp.where(global_marks[:, None], jnp.zeros_like(cotangent), cotangent)
    first_block = shard_index * block_here
    last_block = shard_count * block_here - 1

    def block_step(carried, number):
        begin = number * BLK
        window = lax.dynamic_slice_in_dim(extended, begin, 3 * BLK, 0)
        gathered_keys = jnp.concatenate([window[:, :columns], shared_keys], axis=0).reshape(
            -1, head_here, HEAD_DIM
        )
        gathered_values = jnp.concatenate([window[:, columns:], shared_values], axis=0).reshape(
            -1, head_here, HEAD_DIM
        )
        global_block = first_block + number
        usable = jnp.concatenate(
            [
                jnp.full((BLK,), global_block > 0),
                jnp.ones((BLK,), bool),
                jnp.full((BLK,), global_block < last_block),
                jnp.ones((shared_count,), bool),
            ]
        )
        attention_output, query_gradient_rows, key_gradient_rows, value_gradient_rows = attend(
            lax.dynamic_slice_in_dim(query_rows, begin, BLK, 0).reshape(BLK, head_here, HEAD_DIM),
            gathered_keys,
            gathered_values,
            usable,
            lax.dynamic_slice_in_dim(sparse_cot, begin, BLK, 0).reshape(BLK, head_here, HEAD_DIM),
        )
        key_flat = key_gradient_rows.reshape(-1, columns)
        value_flat = value_gradient_rows.reshape(-1, columns)
        return (
            carried,
            (
                attention_output.reshape(BLK, columns),
                query_gradient_rows.reshape(BLK, columns),
                key_flat[: 3 * BLK],
                value_flat[: 3 * BLK],
                key_flat[3 * BLK :],
                value_flat[3 * BLK :],
            ),
        )

    unused = jnp.zeros((), jnp.float32)
    unused, (sparse_out, sparse_dq, window_dk, window_dv, shared_dk, shared_dv) = lax.scan(
        block_step, unused, jnp.arange(block_here, dtype=jnp.int32)
    )
    sparse_out = sparse_out.reshape(local_count, columns)
    sparse_dq = sparse_dq.reshape(local_count, columns)
    ext_keys = jnp.zeros((local_count + 2 * BLK, columns), jnp.float32)
    ext_values = jnp.zeros((local_count + 2 * BLK, columns), jnp.float32)
    for block_number in range(block_here):
        lower = block_number * BLK
        ext_keys = ext_keys.at[lower : lower + 3 * BLK].add(window_dk[block_number])
        ext_values = ext_values.at[lower : lower + 3 * BLK].add(window_dv[block_number])
    grad_ext = jnp.concatenate([ext_keys, ext_values], axis=1)
    grad_shared = jnp.concatenate([jnp.sum(shared_dk, axis=0), jnp.sum(shared_dv, axis=0)], axis=1)
    softmax_scale_factor = HEAD_DIM ** (-0.5)
    query_per_head = global_query.reshape(global_count, head_here, HEAD_DIM)
    cotangent_head_rows = global_cot.reshape(global_count, head_here, HEAD_DIM)
    key_per_head = key_rows.reshape(local_count, head_here, HEAD_DIM)
    value_per_head = value_rows.reshape(local_count, head_here, HEAD_DIM)
    logit_scores = (
        jnp.einsum("crj,prj->rcp", query_per_head, key_per_head, preferred_element_type=jnp.float32)
        * softmax_scale_factor
    )
    local_max = jnp.max(logit_scores, axis=2)
    local_sum = jnp.sum(jnp.exp(logit_scores - local_max[:, :, None]), axis=2)
    maxima, totals = joined((local_max, local_sum), "seq", merge_stats)
    chances = jnp.exp(logit_scores - maxima[:, :, None]) / totals[:, :, None]
    attention_weight_rows = chances.astype(jnp.bfloat16)
    partial_out = jnp.einsum(
        "bxl,lby->xby", attention_weight_rows, value_per_head, preferred_element_type=jnp.float32
    ).reshape(global_count, columns)
    global_out = lax.psum(partial_out, "seq").astype(jnp.bfloat16)
    deltas = jnp.transpose(
        jnp.sum(
            cotangent_head_rows.astype(jnp.float32)
            * global_out.reshape(global_count, head_here, HEAD_DIM).astype(jnp.float32),
            axis=2,
        )
    )[:, :, None]
    probability_gradient = jnp.einsum(
        "crj,prj->rcp", cotangent_head_rows, value_per_head, preferred_element_type=jnp.float32
    )
    scaled_scores = (chances * (probability_gradient - deltas) * softmax_scale_factor).astype(
        jnp.bfloat16
    )
    global_dq = jnp.einsum(
        "bxl,lby->xby", scaled_scores, key_per_head, preferred_element_type=jnp.float32
    ).reshape(global_count, columns)
    local_dk = jnp.einsum(
        "cgi,gcx->icx", scaled_scores, query_per_head, preferred_element_type=jnp.float32
    ).reshape(local_count, columns)
    local_dv = jnp.einsum(
        "cgi,gcx->icx",
        attention_weight_rows,
        cotangent_head_rows,
        preferred_element_type=jnp.float32,
    ).reshape(local_count, columns)
    global_grads = jnp.concatenate([grad_shared[rounds_count * BLK :], global_dq], axis=1)
    summed = lax.psum(global_grads, "seq")
    owned_rows = lax.dynamic_slice_in_dim(summed, shard_index * global_here, global_here, 0)
    returned = return_grads(
        grad_shared[: rounds_count * BLK].reshape(rounds_count, BLK, 2 * columns),
        partner_mask,
        levels,
    )
    from_next = passed_along(grad_ext[:BLK].astype(jnp.bfloat16), "seq", -1).astype(jnp.float32)
    from_prev = passed_along(grad_ext[BLK + local_count :].astype(jnp.bfloat16), "seq", 1).astype(
        jnp.float32
    )
    own_grads = grad_ext[BLK : BLK + local_count]
    own_grads = own_grads.at[:BLK].add(from_prev).at[local_count - BLK :].add(from_next)
    landing = chosen[0] * BLK
    own_grads = lax.dynamic_update_slice_in_dim(
        own_grads, lax.dynamic_slice_in_dim(own_grads, landing, BLK, 0) + returned[0], landing, 0
    )
    own_grads = own_grads + jnp.concatenate([local_dk, local_dv], axis=1)
    own_grads = own_grads.at[local_pos].add(owned_rows[:, : 2 * columns])
    grad_query_rows = sparse_dq.at[local_pos].add(owned_rows[:, 2 * columns :])
    own_out = lax.dynamic_slice_in_dim(global_out, shard_index * global_here, global_here, 0)
    attention = sparse_out.at[local_pos].set(own_out)
    return (
        attention,
        grad_query_rows.astype(jnp.bfloat16),
        own_grads[:, :columns].astype(jnp.bfloat16),
        own_grads[:, columns:].astype(jnp.bfloat16),
    )


def solution(mesh):
    placed = (P("seq", "tp"), P("seq", "tp"), P("seq", "tp"), P("seq", "tp"), P("seq"), P(), P())
    return jax.shard_map(
        per_device,
        mesh=mesh,
        in_specs=placed,
        out_specs=(P("seq", "tp"), P("seq", "tp"), P("seq", "tp"), P("seq", "tp")),
        check_vma=False,
    )
```

profile of v0, /device:TPU:8, one launch (start us, length us, event | category | flops | bytes accessed | tf_op | source)
XLA Modules:
  0.0 2458.3 jit_solution(18070954303673704445)
XLA Ops:
  16.2 2.2 collective-permute-start.2
  18.4 2.6 collective-permute-start
  21.0 4.0 collective-permute-start.1
  26.8 185.6 %all-gather.8 = bf16[64,4,1024]{2,1,0:T(4,128)(2,1)S(1)} all-gather(bf16[1,4,1024]{2,1,0:T(4,128)(2,1)S(1)} %bitcast.219), channel_id=4, replica_groups=mesh['seq'=64,'tp'=4] {'seq'}, dimensions={0}, use_global_device_ids=true | all-gather | bytes 532480 | tf_op jit(solution)/shard_map/all_gather | solution.py:116
  213.8 183.8 %all-gather.4 = f32[512,256]{1,0:T(8,128)S(1)} all-gather(f32[8,256]{1,0:T(8,128)S(1)} %exponential_reduce_fusion), channel_id=6, replica_groups=mesh['seq'=64,'tp'=4] {'seq'}, dimensions={0}, use_global_device_ids=true | all-gather | bytes 532480 | tf_op jit(solution)/shard_map/all_gather | solution.py:28
  398.4 176.8 %all-gather.3 = f32[512,256]{1,0:T(8,128)S(1)} all-gather(f32[8,256]{1,0:T(8,128)S(1)} %get-tuple-element.345), channel_id=5, replica_groups=mesh['seq'=64,'tp'=4] {'seq'}, dimensions={0}, use_global_device_ids=true | all-gather | bytes 532480 | tf_op jit(solution)/shard_map/all_gather | solution.py:28
  576.1 47.3 %while.40 = (s32[]{:T(128)}, f32[8,256]{1,0:T(8,128)S(1)}, f32[8,256]{1,0:T(8,128)S(1)}, f32[63,8,256]{2,1,0:T(8,128)}, f32[63,8,256]{2,1,0:T(8,128)}, /*index=5*/s32[]{:T(128)}) while((s32[]{:T(128)}, f32[8,256]{1,0:T(8,128)S(1)}, f32[8,256]{1,0:T(8,128)S(1)}, f32[63,8,256]{2,1,0:T(8,128)}, f32[63,8,256]{2,1,0:T(8,128)}, ...), condition=%wide.region_9.10_spmd, body=%wide.region_8.9_spmd.sunk | while | flops 12290 | bytes 49225 | solution.py:31
  625.1 2.0 broadcast_select_fusion.1
  627.1 356.8 %all-reduce.6 = bf16[256,1024]{0,1:T(8,128)(2,1)S(1)} all-reduce(f32[256,1024]{0,1:T(8,128)} %bitcast.212), channel_id=1, replica_groups=mesh['seq'=64,'tp'=4] {'seq'}, use_global_device_ids=true, to_apply=%region_10.11 | all-reduce | flops 262144 | bytes 1572864 | tf_op jit(solution)/shard_map/psum | solution.py:209
  983.9 1.9 gather_fusion.3
  985.8 1.9 broadcast_select_fusion.2
  987.7 192.3 %all-gather.9 = bf16[64,4,1024]{2,1,0:T(4,128)(2,1)} all-gather(bf16[1,4,1024]{2,1,0:T(4,128)(2,1)S(1)} %bitcast.218), channel_id=7, replica_groups=mesh['seq'=64,'tp'=4] {'seq'}, dimensions={0}, use_global_device_ids=true | all-gather | bytes 532480 | tf_op jit(solution)/shard_map/all_gather | solution.py:119
  1186.9 190.6 %all-gather.6 = bf16[64,4,1024]{2,1,0:T(4,128)(2,1)} all-gather(bf16[1,4,1024]{2,1,0:T(4,128)(2,1)S(1)} %bitcast.217), channel_id=2, replica_groups=mesh['seq'=64,'tp'=4] {'seq'}, dimensions={0}, use_global_device_ids=true | all-gather | bytes 532480 | tf_op jit(solution)/shard_map/all_gather | solution.py:118
  1377.5 187.6 %all-gather.7 = bf16[64,4,1024]{2,1,0:T(4,128)(2,1)} all-gather(bf16[1,4,1024]{2,1,0:T(4,128)(2,1)S(1)} %bitcast.216), channel_id=3, replica_groups=mesh['seq'=64,'tp'=4] {'seq'}, dimensions={0}, use_global_device_ids=true | all-gather | bytes 532480 | tf_op jit(solution)/shard_map/all_gather | solution.py:117
  1568.3 19.4 collective-permute-done.5
  1588.6 2.0 copy.128
  1590.7 2.0 reshape.379
  1592.6 2.0 copy.130
  1595.6 2.0 copy.133
  1597.7 3.0 multiply_convert_fusion.1
  1600.7 4.2 collective-permute-done.6
  1605.9 2.8 collective-permute-start.7
  1609.6 2.8 pad_maximum_fusion.4
  1612.4 4.3 collective-permute-done.7
  1618.5 79.3 %while.39 = (s32[]{:T(128)}, bf16[2,128,1024]{2,1,0:T(8,128)(2,1)}, f32[2,128,1024]{2,1,0:T(8,128)}, f32[2,384,1024]{2,1,0:T(8,128)}, f32[2,384,1024]{2,1,0:T(8,...) while((s32[]{:T(128)}, bf16[2,128,1024]{2,1,0:T(8,128)(2,1)}, ...), condition=%wide.region_5.6_spmd, body=%wide.region_1.5_spmd.sunk | while | flops 1226704896 | bytes 130574560 | solution.py:179
  1622.7 1.9 constant_dynamic-slice_fusion.9
  1626.5 2.9 fusion.107
  1629.3 2.1 fusion.108
  1637.0 2.9 constant_dynamic-update-slice_fusion.15
  1644.4 2.0 fusion.110
  1646.4 3.0 copy.203
  1649.4 2.9 constant_dynamic-update-slice_fusion.14
  1662.3 1.9 constant_dynamic-slice_fusion.9
  1666.1 2.9 fusion.107
  1668.9 2.1 fusion.108
  1676.6 2.9 constant_dynamic-update-slice_fusion.15
  1684.0 2.0 fusion.110
  1686.0 3.0 copy.203
  1689.0 2.9 constant_dynamic-update-slice_fusion.14
  1697.8 2.3 reduce_sum.55
  1700.5 2.3 reduce_sum.56
  1704.4 2.1 convert_bitcast_fusion
  1709.3 2.6 copy.159
  1711.9 2.5 copy.160
  1714.5 2.5 fusion.52
  1717.0 2.6 copy.150
  1723.5 8.3 collective-permute-done.11
  1731.8 2.2 fusion.22
  1736.1 1.9 pad_maximum_fusion.3
  1738.0 5.5 collective-permute-done.12
  1745.3 3.0 fusion.15
  1748.7 11.7 collective-permute-done.13
  1761.4 2.8 collective-permute-start.14
  1765.3 2.0 collective-permute-start.8
  1768.9 4.7 collective-permute-start.9
  1773.6 2.5 scatter_fusion
  1776.2 3.7 collective-permute-done.14
  1781.3 1.9 collective-permute-start.15
  1783.1 2.1 fusion.19
  1785.3 2.5 fusion.20
  1787.8 4.2 collective-permute-done.15
  1792.0 2.7 fusion.21
  1794.7 1.9 maximum_add_fusion
  1796.7 649.4 %all-reduce.5.cloned.1.call-done = f32[256,3072]{1,0:T(8,128)} async-done(((f32[256,3072]{1,0:T(8,128)}), f32[256,3072]{1,0:T(8,128)}) %all-reduce.5.cloned.1.call-update) | async-done | bytes 3145744 | tf_op jit(solution)/shard_map/psum | solution.py:236
  (305 shorter events, 139.0 us)
Async XLA Ops:
  7.2 2438.9 %all-reduce.5.cloned.1.call-start = ((), (), s32[]{:S(2)}) async-start(), calls=%async_computation | async-start | bytes 6291456 | tf_op jit(solution)/shard_map/psum | solution.py:236
  11.7 1598.0 %copy-start.16 = (bf16[256,1024]{0,1:T(8,128)(2,1)}, bf16[256,1024]{0,1:T(8,128)(2,1)S(1)}, u32[]{:S(2)}) copy-start(bf16[256,1024]{0,1:T(8,128)(2,1)S(1)} %copy.125) | copy-start | bytes 1572868
  13.1 199.3 %copy-start.23 = (bf16[256,1024]{0,1:T(8,128)(2,1)}, bf16[256,1024]{0,1:T(8,128)(2,1)S(1)}, u32[]{:S(2)}) copy-start(bf16[256,1024]{0,1:T(8,128)(2,1)S(1)} %copy.126) | copy-start | bytes 1572868
  13.1 11.9 copy-start.43
  16.2 608.8 %collective-permute-start.2 = (bf16[1,128,2048]{2,1,0:T(8,128)(2,1)}, bf16[1,128,2048]{2,1,0:T(8,128)(2,1)}, u32[]{:S(2)}, u32[]{:S(2)}) collective-permute-start(bf16[1,128,2048]{2,1,0:T(8,128)(2,1)} %bitcast.27), channel_id=1, source_target_pairs={{0,4},{4,0},{8,12},{12,8},{16,20},{20,16},{24,28},{28,24},{32,36},... | collective-permute-start | bytes 1572872 | tf_op jit(solution)/shard_map/ppermute | solution.py:11
  18.4 1591.2 %collective-permute-start = (bf16[128,2048]{0,1:T(8,128)(2,1)}, bf16[128,2048]{0,1:T(8,128)(2,1)}, u32[]{:S(2)}, u32[]{:S(2)}) collective-permute-start(bf16[128,2048]{0,1:T(8,128)(2,1)} %get-tuple-element.341), channel_id=1, source_target_pairs={{0,4},{4,8},{8,12},{12,16},{16,20},{20,24},{24,28},{28,32},{32,36}... | collective-permute-start | bytes 1572872 | tf_op jit(solution)/shard_map/ppermute | solution.py:21
  21.0 1588.6 %collective-permute-start.1 = (bf16[128,2048]{0,1:T(8,128)(2,1)}, bf16[128,2048]{0,1:T(8,128)(2,1)}, u32[]{:S(2)}, u32[]{:S(2)}) collective-permute-start(bf16[128,2048]{0,1:T(8,128)(2,1)} %get-tuple-element.342), channel_id=1, source_target_pairs={{4,0},{8,4},{12,8},{16,12},{20,16},{24,20},{28,24},{32,28},{36,32}... | collective-permute-start | bytes 1572872 | tf_op jit(solution)/shard_map/ppermute | solution.py:22
  25.1 1.7 copy-start.41
  397.6 225.9 %copy-start.37 = (bf16[256,1024]{1,0:T(8,128)(2,1)S(1)}, bf16[256,1024]{1,0:T(8,128)(2,1)}, u32[]{:S(2)}) copy-start(bf16[256,1024]{1,0:T(8,128)(2,1)} %param.25) | copy-start | bytes 1572868
  627.1 358.7 %collective-permute-start.3 = (bf16[1,128,2048]{2,1,0:T(8,128)(2,1)}, bf16[1,128,2048]{2,1,0:T(8,128)(2,1)}, u32[]{:S(2)}, u32[]{:S(2)}) collective-permute-start(bf16[1,128,2048]{2,1,0:T(8,128)(2,1)} %broadcast_select_fusion.1), channel_id=1, source_target_pairs={{0,8},{4,12},{8,0},{12,4},{16,24},{20,28},{24,16},{28,20},{32,40},... | collective-permute-start | bytes 1572872 | tf_op jit(solution)/shard_map/ppermute | solution.py:11
  983.9 199.5 %copy-start.30 = (bf16[256,1024]{0,1:T(8,128)(2,1)}, bf16[256,1024]{0,1:T(8,128)(2,1)S(1)}, u32[]{:S(2)}) copy-start(bf16[256,1024]{0,1:T(8,128)(2,1)S(1)} %all-reduce.6) | copy-start | bytes 1572868
  987.7 577.4 %collective-permute-start.4 = (bf16[1,128,2048]{2,1,0:T(8,128)(2,1)}, bf16[1,128,2048]{2,1,0:T(8,128)(2,1)}, u32[]{:S(2)}, u32[]{:S(2)}) collective-permute-start(bf16[1,128,2048]{2,1,0:T(8,128)(2,1)} %broadcast_select_fusion.2), channel_id=1, source_target_pairs={{0,16},{4,20},{8,24},{12,28},{16,0},{20,4},{24,8},{28,12},{32,48},... | collective-permute-start | bytes 1572872 | tf_op jit(solution)/shard_map/ppermute | solution.py:11
  1186.9 379.4 %copy-start.26 = (f32[256,8,128]{2,1,0:T(8,128)S(1)}, f32[256,8,128]{2,1,0:T(8,128)}, u32[]{:S(2)}) copy-start(f32[256,8,128]{2,1,0:T(8,128)} %copy.145) | copy-start | bytes 3145732
  1186.9 379.8 %copy-start.38 = (bf16[256,8,128]{0,2,1:T(8,128)(2,1)S(1)}, bf16[256,8,128]{0,2,1:T(8,128)(2,1)}, u32[]{:S(2)}) copy-start(bf16[256,8,128]{0,2,1:T(8,128)(2,1)} %copy.157) | copy-start | bytes 1572868
  1566.2 21.4 collective-permute-start.5
  1587.7 7.0 copy-start.34
  1588.5 16.3 collective-permute-start.6
  1597.7 11.1 copy-start.35
  1600.7 9.0 copy-start.24
  1605.9 10.8 collective-permute-start.7
  1619.8 1.6 copy-start.11
  1619.8 1.7 copy-start.12
  1622.7 8.8 copy-start
  1625.7 3.6 copy-start.8
  1637.0 2.9 copy-start.2
  1637.0 4.1 copy-start.4
  1639.9 2.0 copy-start.1
  1642.0 1.9 copy-start.9
  1649.4 2.9 copy-start.3
  1654.9 2.3 copy-start.39
  1659.4 1.7 copy-start.12
  1662.3 8.8 copy-start
  1665.3 3.6 copy-start.8
  1676.6 3.0 copy-start.2
  1676.6 4.3 copy-start.4
  1679.6 2.0 copy-start.1
  1681.6 1.9 copy-start.9
  1689.0 2.9 copy-start.3
  1694.6 2.3 copy-start.39
  1704.4 3.5 copy-start.22
  1704.4 3.5 copy-start.25
  1706.5 13.4 collective-permute-start.10
  1709.3 5.1 copy-start.17
  1717.0 2.6 copy-start.31
  1721.0 2.4 copy-start.32
  1721.1 10.8 collective-permute-start.11
  1723.5 10.5 copy-start.15
  1731.8 2.2 copy-start.33
  1734.0 9.5 collective-permute-start.12
  1738.0 7.3 copy-start.5
  1745.2 15.2 copy-start.13
  1745.2 15.2 collective-permute-start.13
  1748.3 19.0 copy-start.6
  1760.4 4.8 copy-start.19
  1761.4 18.4 collective-permute-start.14
  1765.3 8.3 copy-start.42
  1765.3 14.6 copy-start.14
  1765.3 17.8 collective-permute-start.8
  1768.9 16.4 collective-permute-start.9
  1776.2 7.0 copy-start.7
  1781.3 10.8 collective-permute-start.15
  1785.3 6.8 copy-start.20
  1787.8 6.9 copy-start.27
  1787.8 6.9 copy-start.28
  (10 other events, 10.6 us)
Sparse Core Ops, SparseCore 0:
  1738.2 707.8 all-reduce.4
where the time goes:
time: 2470 us; the launch traced here: 2460 us
  blocking collectives  1470 us (60%)
  waiting for transfers between devices  711 us (29%)
  other arithmetic  102 us (4%)
  local copies, waits for them, and re-layouts  100 us (4%)
  matrix products  26.1 us (1%)
  starting transfers between devices  24.7 us (1%)
    psum x1, waiting for transfers between devices, per_device(): summed = lax.psum(global_grads, 'seq')  649 us
    all_gather x2, blocking collectives, joined(): pieces = jax.tree.map(lambda part: lax.all_gather(part, axis), value)  361 us
    psum x1, blocking collectives, per_device(): global_out = lax.psum(partial_out, 'seq').astype(jnp.bfloat16)  357 us
    all_gather x1, blocking collectives, per_device(): lax.all_gather(cotangent[local_pos], 'seq', axis=0, tiled=True)  192 us
    all_gather x1, blocking collectives, per_device(): lax.all_gather(value_rows[local_pos], 'seq', axis=0, tiled=True)  191 us
    all_gather x1, blocking collectives, per_device(): lax.all_gather(key_rows[local_pos], 'seq', axis=0, tiled=True)  188 us
    all_gather x1, blocking collectives, per_device(): lax.all_gather(query_rows[local_pos], 'seq', axis=0, tiled=True)  186 us
    ppermute x12, waiting for transfers between devices, from_partner(): lax.ppermute(shard, axis, [(i, i ^ 1 << bit) for i in range(lax.axis_size...  61.3 us
  transfers between devices with their start and end apart: 17, of which 9 were waited for; matrix products, arithmetic and copies ran while one was open for 5% of the time, Pallas kernels for 0%

commit v1 on v0

v1 whole, which is shorter than its diff:
```python
import functools

import jax
import jax.numpy as jnp
from jax import lax
from jax.experimental import pallas as pl
from jax.experimental.pallas import tpu as pltpu
from jax.sharding import PartitionSpec as P

HEAD_DIM = 128
BLK = 128
NX, NZ, NY = 2, 8, 4
NP = NX * NY
SCALE = HEAD_DIM**-0.5
MESH = pl.DeviceIdType.MESH
F32 = jnp.float32
BF16 = jnp.bfloat16


def nt(a, b):
    return lax.dot_general(a, b, (((1,), (1,)), ((), ())), preferred_element_type=F32)


def nn(a, b):
    return lax.dot_general(a, b, (((1,), (0,)), ((), ())), preferred_element_type=F32)


def tn(a, b):
    return lax.dot_general(a, b, (((0,), (0,)), ((), ())), preferred_element_type=F32)


def place():
    me = lax.axis_index("seq")
    return me, me // (NZ * NY), (me // NY) % NZ, me % NY


def seq_of(x, z, y):
    return (x * NZ + z) * NY + y


def greet(peers):
    barrier = pltpu.get_barrier_semaphore()
    for peer in peers:
        pl.semaphore_signal(barrier, inc=1, device_id=peer, device_id_type=MESH)
    pl.semaphore_wait(barrier, len(peers))


def plane_peers(x, z, y, tp):
    peers = []
    for offset in range(1, NP):
        dx, dy = offset // NY, offset % NY
        px, py = lax.rem(x + dx, NX), lax.rem(y + dy, NY)
        peers.append((offset, px * NY + py, (seq_of(px, z, py), tp)))
    return peers


def ring_peers(x, z, y, tp):
    return (seq_of(x, lax.rem(z + 1, NZ), y), tp), (seq_of(x, lax.rem(z + NZ - 1, NZ), y), tp)


def line_peers(me, tp):
    return (lax.rem(me + 1, NX * NZ * NY), tp), (lax.rem(me + NX * NZ * NY - 1, NX * NZ * NY), tp)


def remote(src, dst, send, recv, device):
    return pltpu.make_async_remote_copy(
        src_ref=src, dst_ref=dst, send_sem=send, recv_sem=recv, device_id=device, device_id_type=MESH
    )


def steps_of(array):
    return (4, 3) if array < 2 else (3, 4)


def gather_kernel(
    q_ref, k_ref, v_ref, c_ref, pos_ref, gath_ref, prev_ref, next_ref,
    piece_ref, plane_send, plane_recv, ring_send, ring_recv, edge_send, edge_recv,
):
    me, x, z, y = place()
    tp = lax.axis_index("tp")
    peers = plane_peers(x, z, y, tp)
    right, left = ring_peers(x, z, y, tp)
    after, before = line_peers(me, tp)
    mine = x * NY + y

    rows = lax.broadcasted_iota(jnp.int32, (16, 256), 0)
    columns = lax.broadcasted_iota(jnp.int32, (16, 256), 1)
    hit = columns == pos_ref[...]
    total = jnp.zeros((16, q_ref.shape[1]), F32)
    for number, ref in enumerate((q_ref, k_ref, v_ref, c_ref)):
        pick = jnp.where(hit & (rows // 4 == number), 1.0, 0.0).astype(BF16)
        total = total + nn(pick, ref[...])
    piece_ref[mine] = total.astype(BF16)

    greet([peer for _, _, peer in peers] + [right, left, after, before])
    copies = []
    for offset, _, peer in peers:
        copy = remote(
            piece_ref.at[mine], piece_ref.at[mine], plane_send.at[offset], plane_recv.at[offset], peer
        )
        copy.start()
        copies.append(copy)
    edges = []
    for number, ref in enumerate((k_ref, v_ref)):
        edges.append(
            remote(ref.at[pl.ds(BLK, BLK)], prev_ref.at[number], edge_send.at[number], edge_recv.at[number], after)
        )
        edges.append(
            remote(ref.at[pl.ds(0, BLK)], next_ref.at[number], edge_send.at[2 + number], edge_recv.at[2 + number], before)
        )
    for copy in copies:
        copy.wait()

    out_row = lax.broadcasted_iota(jnp.int32, (32, 128), 0)
    in_row = lax.broadcasted_iota(jnp.int32, (32, 128), 1)
    pieces = piece_ref[...].reshape(128, -1)
    for number in range(4):
        pick = jnp.where(in_row == (out_row // 4) * 16 + number * 4 + out_row % 4, 1.0, 0.0)
        gath_ref[z, number] = nn(pick.astype(BF16), pieces).astype(BF16)

    def hop(way, step, number):
        shift = lax.rem(z + NZ - step + 1, NZ) if way == 0 else lax.rem(z + step - 1, NZ)
        slot = (way * 4 + step - 1) * 4 + number
        part = gath_ref.at[shift, number]
        return remote(part, part, ring_send.at[slot], ring_recv.at[slot], right if way == 0 else left)

    flying = {}
    for number in range(4):
        for way in range(2):
            flying[way, 1, number] = hop(way, 1, number)
            flying[way, 1, number].start()
    for edge in edges:
        edge.start()
    for step in range(1, 5):
        for number in range(4):
            for way in range(2):
                if step <= steps_of(number)[way]:
                    flying[way, step, number].wait_recv()
                    if step < steps_of(number)[way]:
                        flying[way, step + 1, number] = hop(way, step + 1, number)
                        flying[way, step + 1, number].start()
    for copy in flying.values():
        copy.wait_send()
    for edge in edges:
        edge.wait()


def attend_kernel(
    q_ref, k_ref, v_ref, c_ref, keep_ref, bias_ref, prev_ref, next_ref, rand_ref, gath_ref,
    out_ref, dq_ref, dk_ref, dv_ref, edge_ref, drand_ref, part_ref,
    stat_ref, ring_ref, mid_ref, plane_ref, ring_send, ring_recv, plane_send, plane_recv,
):
    me, x, z, y = place()
    tp = lax.axis_index("tp")
    peers = plane_peers(x, z, y, tp)
    mine = x * NY + y
    rings = [(offset, (seq_of(x, lax.rem(z + offset, NZ), y), tp)) for offset in range(1, NZ)]
    heads = q_ref.shape[1] // HEAD_DIM

    def head_columns(head):
        return pl.ds(pl.multiple_of(head * HEAD_DIM, HEAD_DIM), HEAD_DIM)

    def gathered(number, columns):
        return gath_ref[:, number, :, columns].reshape(256, HEAD_DIM)

    def global_stats(head, carry):
        columns = head_columns(head)
        scores = nt(k_ref[:, columns], gathered(0, columns)) * SCALE
        slopes = nt(v_ref[:, columns], gathered(3, columns))
        top = jnp.max(scores, axis=0, keepdims=True)
        raised = jnp.exp(scores - top)
        stat_ref[0, pl.ds(head, 1), :] = top
        stat_ref[1, pl.ds(head, 1), :] = jnp.sum(raised, axis=0, keepdims=True)
        stat_ref[2, pl.ds(head, 1), :] = jnp.sum(raised * slopes, axis=0, keepdims=True)
        return carry

    lax.fori_loop(0, heads, global_stats, 0)

    def join(ref):
        top = ref[0, 0]
        for number in range(1, 8):
            top = jnp.maximum(top, ref[number, 0])
        total = jnp.zeros_like(top)
        slope = jnp.zeros_like(top)
        for number in range(8):
            factor = jnp.exp(ref[number, 0] - top)
            total = total + ref[number, 1] * factor
            slope = slope + ref[number, 2] * factor
        return top, total, slope

    greet([peer for _, _, peer in peers] + [peer for _, peer in rings])
    ring_copies = []
    for offset, peer in rings:
        copy = remote(stat_ref, ring_ref.at[offset], ring_send.at[offset], ring_recv.at[offset], peer)
        copy.start()
        ring_copies.append(copy)
    ring_ref[0] = stat_ref[...]

    def sparse(head, carry):
        columns = head_columns(head)
        queries = q_ref[:, columns]
        cots = jnp.where(keep_ref[...] > 0.5, c_ref[:, columns], jnp.zeros((256, HEAD_DIM), BF16))
        keys = jnp.concatenate([k_ref[:, columns], rand_ref[0, :, columns], gathered(1, columns)], axis=0)
        values = jnp.concatenate([v_ref[:, columns], rand_ref[1, :, columns], gathered(2, columns)], axis=0)
        edge_keys = (prev_ref[0, :, columns], next_ref[0, :, columns])
        edge_values = (prev_ref[1, :, columns], next_ref[1, :, columns])
        halves = (queries[:BLK], queries[BLK:])
        cot_halves = (cots[:BLK], cots[BLK:])
        main = nt(keys, queries) * SCALE
        edge = (
            jnp.concatenate([nt(edge_keys[i], halves[i]) for i in range(2)], axis=1) * SCALE + bias_ref[...]
        )
        top = jnp.maximum(jnp.max(main, axis=0, keepdims=True), jnp.max(edge, axis=0, keepdims=True))
        main = jnp.exp(main - top)
        edge = jnp.exp(edge - top)
        inverse = 1.0 / (jnp.sum(main, axis=0, keepdims=True) + jnp.sum(edge, axis=0, keepdims=True))
        main = main * inverse
        edge = edge * inverse
        main_w = main.astype(BF16)
        edge_w = edge.astype(BF16)
        main_g = nt(values, cots)
        edge_g = jnp.concatenate([nt(edge_values[i], cot_halves[i]) for i in range(2)], axis=1)
        delta = jnp.sum(main * main_g, axis=0, keepdims=True) + jnp.sum(edge * edge_g, axis=0, keepdims=True)
        main_s = (main * (main_g - delta) * SCALE).astype(BF16)
        edge_s = (edge * (edge_g - delta) * SCALE).astype(BF16)
        sides = [slice(0, BLK), slice(BLK, 2 * BLK)]
        out = tn(main_w, values) + jnp.concatenate(
            [tn(edge_w[:, sides[i]], edge_values[i]) for i in range(2)], axis=0
        )
        out_ref[:, columns] = out.astype(BF16)
        dq_ref[:, columns] = tn(main_s, keys) + jnp.concatenate(
            [tn(edge_s[:, sides[i]], edge_keys[i]) for i in range(2)], axis=0
        )
        dkeys = nn(main_s, queries)
        dvalues = nn(main_w, cots)
        dk_ref[:, columns] = dkeys[:256]
        dv_ref[:, columns] = dvalues[:256]
        drand_ref[0, :, columns] = dkeys[256:384].astype(BF16)
        drand_ref[1, :, columns] = dvalues[256:384].astype(BF16)
        part_ref[:, 2, :, columns] = dkeys[384:].astype(BF16).reshape(NZ, 32, HEAD_DIM)
        part_ref[:, 3, :, columns] = dvalues[384:].astype(BF16).reshape(NZ, 32, HEAD_DIM)
        for i in range(2):
            edge_ref[i, 0, :, columns] = nn(edge_s[:, sides[i]], halves[i]).astype(BF16)
            edge_ref[i, 1, :, columns] = nn(edge_w[:, sides[i]], cot_halves[i]).astype(BF16)
        return carry

    lax.fori_loop(0, heads // 2, sparse, 0)
    for copy in ring_copies:
        copy.wait()
    for number, value in enumerate(join(ring_ref)):
        mid_ref[number] = value
    plane_ref[0] = mid_ref[...]
    plane_copies = []
    for offset, _, peer in peers:
        copy = remote(mid_ref, plane_ref.at[offset], plane_send.at[offset], plane_recv.at[offset], peer)
        copy.start()
        plane_copies.append(copy)
    lax.fori_loop(heads // 2, heads, sparse, 0)
    for copy in plane_copies:
        copy.wait()
    top, total, slope = join(plane_ref)
    inverse = 1.0 / total
    stat_ref[0] = top
    stat_ref[1] = inverse
    stat_ref[2] = slope * inverse

    def global_grads(head, carry):
        columns = head_columns(head)
        keys, values = k_ref[:, columns], v_ref[:, columns]
        queries, cots = gathered(0, columns), gathered(3, columns)
        row = pl.ds(head, 1)
        probs = jnp.exp(nt(keys, queries) * SCALE - stat_ref[0, row, :]) * stat_ref[1, row, :]
        slopes = nt(values, cots)
        scores = (probs * (slopes - stat_ref[2, row, :]) * SCALE).astype(BF16)
        weights = probs.astype(BF16)
        dk_ref[:, columns] += nn(scores, queries)
        dv_ref[:, columns] += nn(weights, cots)
        part_ref[:, 0, :, columns] = tn(scores, keys).astype(BF16).reshape(NZ, 32, HEAD_DIM)
        part_ref[:, 1, :, columns] = tn(weights, values).astype(BF16).reshape(NZ, 32, HEAD_DIM)
        return carry

    lax.fori_loop(0, heads, global_grads, 0)


def reduce_kernel(
    part_ref, edge_ref, total_ref, first_ref, last_ref,
    out_ring, in_ring, out_piece, in_piece, ring_send, ring_recv, plane_send, plane_recv, edge_send, edge_recv,
):
    me, x, z, y = place()
    tp = lax.axis_index("tp")
    peers = plane_peers(x, z, y, tp)
    right, left = ring_peers(x, z, y, tp)
    after, before = line_peers(me, tp)
    mine = x * NY + y
    greet([peer for _, _, peer in peers] + [right, left, after, before])

    def hop(way, step, number):
        far = steps_of(number)[way] - step + 1
        target = lax.rem(z + far, NZ) if way == 0 else lax.rem(z + NZ - far, NZ)
        slot = (way * 4 + step - 1) * 4 + number
        if step == 1:
            source = part_ref.at[target, number]
        else:
            source = out_ring.at[way, step - 1, number]
            source[...] = (
                part_ref[target, number].astype(F32) + in_ring[way, step - 2, number].astype(F32)
            ).astype(BF16)
        return remote(
            source, in_ring.at[way, step - 1, number], ring_send.at[slot], ring_recv.at[slot],
            right if way == 0 else left,
        )

    flying = {}
    for number in (2, 3, 0, 1):
        for way in range(2):
            flying[way, 1, number] = hop(way, 1, number)
            flying[way, 1, number].start()
    edges = []
    for number in range(2):
        edges.append(
            remote(edge_ref.at[1, number], first_ref.at[number], edge_send.at[number], edge_recv.at[number], after)
        )
        edges.append(
            remote(edge_ref.at[0, number], last_ref.at[number], edge_send.at[2 + number], edge_recv.at[2 + number], before)
        )
    for edge in edges:
        edge.start()
    sums = [None] * 4
    for step in range(1, 5):
        for number in (2, 3, 0, 1):
            for way in range(2):
                if step <= steps_of(number)[way]:
                    flying[way, step, number].wait_recv()
                    if step < steps_of(number)[way]:
                        flying[way, step + 1, number] = hop(way, step + 1, number)
                        flying[way, step + 1, number].start()
    for number in range(4):
        steps = steps_of(number)
        sums[number] = (
            part_ref[z, number].astype(F32)
            + in_ring[0, steps[0] - 1, number].astype(F32)
            + in_ring[1, steps[1] - 1, number].astype(F32)
        ).astype(BF16)
    stacked = jnp.concatenate(sums, axis=0)
    out_row = lax.broadcasted_iota(jnp.int32, (128, 128), 0)
    in_row = lax.broadcasted_iota(jnp.int32, (128, 128), 1)
    source_row = ((out_row % 16) // 4) * 32 + (out_row // 16) * 4 + out_row % 4
    order = jnp.where(in_row == source_row, 1.0, 0.0).astype(BF16)
    out_piece[...] = nn(order, stacked).astype(BF16).reshape(NP, 16, -1)
    copies = []
    for offset, number, peer in peers:
        copy = remote(
            out_piece.at[number], in_piece.at[offset], plane_send.at[offset], plane_recv.at[offset], peer
        )
        copy.start()
        copies.append(copy)
    total = out_piece[mine].astype(F32)
    for copy in copies:
        copy.wait()
    for offset in range(1, NP):
        total = total + in_piece[offset].astype(F32)
    total_ref[...] = total
    for copy in flying.values():
        copy.wait_send()
    for edge in edges:
        edge.wait()


def finish_kernel(
    out_ref, dq_ref, dk_ref, dv_ref, total_ref, first_ref, last_ref, rand_ref, pos_ref, keep_ref, land_ref,
    attention_ref, gq_ref, gk_ref, gv_ref,
):
    rows = lax.broadcasted_iota(jnp.int32, (256, 16), 0)
    columns = lax.broadcasted_iota(jnp.int32, (256, 16), 1)
    hit = rows == pos_ref[...]
    total = total_ref[...]
    high = total.astype(BF16)
    low = (total - high.astype(F32)).astype(BF16)

    def rows_of(number, with_low):
        pick = jnp.where(hit & (columns // 4 == number), 1.0, 0.0).astype(BF16)
        placed = nn(pick, high)
        return placed + nn(pick, low) if with_low else placed

    gq_ref[...] = (dq_ref[...] + rows_of(0, True)).astype(BF16)
    attention_ref[...] = jnp.where(keep_ref[...] > 0.5, out_ref[...], rows_of(1, False).astype(BF16))
    landing = land_ref[...]
    for number, (own_ref, grad_ref) in enumerate(((dk_ref, gk_ref), (dv_ref, gv_ref))):
        back = rand_ref[number].astype(F32)
        edges = jnp.concatenate(
            [first_ref[number].astype(F32), last_ref[number].astype(F32)], axis=0
        )
        borrowed = jnp.concatenate([back, back], axis=0) * landing
        grad_ref[...] = (own_ref[...] + edges + borrowed + rows_of(2 + number, True)).astype(BF16)


VMEM = pl.BlockSpec(memory_space=pltpu.VMEM)
DMA = pltpu.SemaphoreType.DMA


def exchanged(parcel, mask):
    size = lax.axis_size("seq")

    def by(flip):
        return lambda block: lax.ppermute(block, "seq", [(i, i ^ flip) for i in range(size)])

    return lax.switch(mask - 1, [by(flip) for flip in range(1, size)], parcel)


def params(collective_id=None):
    return pltpu.CompilerParams(
        collective_id=collective_id,
        has_side_effects=collective_id is not None,
        vmem_limit_bytes=56 * 1024 * 1024,
    )


def per_device(query_rows, key_rows, value_rows, cotangent, global_pos, partner_mask, rand_block):
    count, columns = query_rows.shape
    me = lax.axis_index("seq")
    shards = lax.axis_size("seq")
    local_pos = global_pos - me * count
    pos_col = jnp.tile(local_pos, 4)[:, None]
    token = jnp.arange(count, dtype=jnp.int32)
    keep = jnp.where(jnp.any(token[:, None] == local_pos[None, :], axis=1, keepdims=True), 0.0, 1.0).astype(F32)
    closed = ((token < BLK) & (me == 0)) | ((token >= BLK) & (me == shards - 1))
    bias = jnp.where(closed, -1e30, 0.0).astype(F32)[None, :]
    chosen = rand_block[0, jnp.bitwise_xor(me, partner_mask[0])]
    landing = jnp.where(token // BLK == chosen, 1.0, 0.0).astype(F32)[:, None]

    def shape(*dims, dtype=BF16):
        return jax.ShapeDtypeStruct(dims, dtype)

    gath, prev, following = pl.pallas_call(
        gather_kernel,
        out_shape=(shape(NZ, 4, 32, columns), shape(2, BLK, columns), shape(2, BLK, columns)),
        in_specs=[VMEM] * 5,
        out_specs=(VMEM,) * 3,
        scratch_shapes=[
            pltpu.VMEM((NP, 16, columns), BF16), DMA((8,)), DMA((8,)), DMA((32,)), DMA((32,)), DMA((4,)), DMA((4,)),
        ],
        compiler_params=params(0),
    )(query_rows, key_rows, value_rows, cotangent, pos_col)

    outgoing = jnp.stack(
        [
            lax.dynamic_slice_in_dim(key_rows, chosen * BLK, BLK, 0),
            lax.dynamic_slice_in_dim(value_rows, chosen * BLK, BLK, 0),
        ]
    )
    borrowed = exchanged(outgoing, partner_mask[0])

    out, dq, dk, dv, edge, drand, part = pl.pallas_call(
        attend_kernel,
        out_shape=(
            shape(count, columns), shape(count, columns, dtype=F32), shape(count, columns, dtype=F32),
            shape(count, columns, dtype=F32), shape(2, 2, BLK, columns), shape(2, BLK, columns),
            shape(NZ, 4, 32, columns),
        ),
        in_specs=[VMEM] * 10,
        out_specs=(VMEM,) * 7,
        scratch_shapes=[
            pltpu.VMEM((3, 8, 256), F32), pltpu.VMEM((8, 3, 8, 256), F32), pltpu.VMEM((3, 8, 256), F32),
            pltpu.VMEM((8, 3, 8, 256), F32), DMA((8,)), DMA((8,)), DMA((8,)), DMA((8,)),
        ],
        compiler_params=params(1),
    )(query_rows, key_rows, value_rows, cotangent, keep, bias, prev, following, borrowed, gath)

    total, first, last = pl.pallas_call(
        reduce_kernel,
        out_shape=(shape(16, columns, dtype=F32), shape(2, BLK, columns), shape(2, BLK, columns)),
        in_specs=[VMEM] * 2,
        out_specs=(VMEM,) * 3,
        scratch_shapes=[
            pltpu.VMEM((2, 4, 4, 32, columns), BF16), pltpu.VMEM((2, 4, 4, 32, columns), BF16),
            pltpu.VMEM((NP, 16, columns), BF16), pltpu.VMEM((NP, 16, columns), BF16),
            DMA((32,)), DMA((32,)), DMA((8,)), DMA((8,)), DMA((4,)), DMA((4,)),
        ],
        compiler_params=params(2),
    )(part, edge)

    returned = exchanged(drand, partner_mask[0])

    width = 256
    wide = lambda *lead: pl.BlockSpec((*lead, width), lambda i: (*([0] * len(lead)), i))
    whole = lambda *dims: pl.BlockSpec(dims, lambda i: (0,) * len(dims))
    return pl.pallas_call(
        finish_kernel,
        grid=(columns // width,),
        out_shape=(shape(count, columns),) * 4,
        in_specs=[
            wide(count), wide(count), wide(count), wide(count), wide(16), wide(2, BLK), wide(2, BLK),
            wide(2, BLK), whole(1, 16), whole(count, 1), whole(count, 1),
        ],
        out_specs=(wide(count),) * 4,
        compiler_params=params(),
    )(out, dq, dk, dv, total, first, last, returned, pos_col.reshape(1, 16), keep, landing)


def solution(mesh):
    placed = (P("seq", "tp"),) * 4 + (P("seq"), P(), P())
    return jax.shard_map(
        per_device,
        mesh=mesh,
        in_specs=placed,
        out_specs=(P("seq", "tp"),) * 4,
        check_vma=False,
    )
```

time: 2470 us -> 281 us (0.11)
  blocking collectives: 1470 us -> 0 us
  waiting for transfers between devices: 711 us -> 59.5 us
  Pallas kernels: 0 us -> 162 us
  other arithmetic: 102 us -> 2.04 us
  local copies, waits for them, and re-layouts: 100 us -> 3.75 us
  loops' own time: 4.07 us -> 30.7 us
  matrix products: 26.1 us -> 0 us
    all_gather x6 -> x0, blocking collectives: 1120 us -> none  [the longest x2 361 us: joined(): pieces = jax.tree.map(lambda part: lax.all_gather(part, axis), value)]
    psum x1 -> x0, waiting for transfers between devices: 649 us -> none  [per_device(): summed = lax.psum(global_grads, 'seq')]
    psum x1 -> x0, blocking collectives: 357 us -> none  [per_device(): global_out = lax.psum(partial_out, 'seq').astype(jnp.bfloat16)]
    pallas_call x0 -> x4, Pallas kernels: none -> 162 us  [the longest x1 56.7 us: per_device(): pl.pallas_call(reduce_kernel, out_shape=(shape(16, columns, dtype=F32), s...]
    add x64 -> x0, other arithmetic: 48.2 us -> none  [the longest x63 46.3 us: merge_stats(): first[1] * jnp.exp(first[0] - maxima)]
    dynamic_update_slice x20 -> x0, local copies, waits for them, and re-layouts: 30.8 us -> none  [per_device(): lax.scan(block_step, unused, jnp.arange(block_here, dtype=jnp.int32))]
    another operation x2, loops' own time: 4.07 us -> 30.7 us  [exchanged(): return lax.switch(mask - 1, [by(flip) for flip in range(1, size)], parcel)]
    ppermute x16 -> x2, waiting for transfers between devices: 61.3 us -> 59.5 us  [by(): lax.ppermute(block, 'seq', [(i, i ^ flip) for i in range(size)])]
  transfers between devices with their start and end apart: 17 -> 2, of which waited for: 9 -> 2; matrix products, arithmetic and copies ran while one was open for 5% -> 0% of each run, Pallas kernels for 0% -> 0%
where the time goes in v1:
time: 281 us; the launch traced here: 282 us
  Pallas kernels  162 us (58%)
  waiting for transfers between devices  59.5 us (21%)
  loops' own time  30.7 us (11%)
  starting transfers between devices  21.3 us (8%)
  local copies, waits for them, and re-layouts  3.75 us (1%)
    ppermute x2, waiting for transfers between devices, by(): lax.ppermute(block, 'seq', [(i, i ^ flip) for i in range(size)])  59.5 us
    pallas_call x1, Pallas kernels, per_device(): pl.pallas_call(reduce_kernel, out_shape=(shape(16, columns, dtype=F32), s...  56.7 us
    pallas_call x1, Pallas kernels, per_device(): pl.pallas_call(attend_kernel, out_shape=(shape(count, columns), shape(cou...  53.7 us
    pallas_call x1, Pallas kernels, per_device(): pl.pallas_call(gather_kernel, out_shape=(shape(NZ, 4, 32, columns), shape...  46.3 us
    another operation x2, loops' own time, exchanged(): return lax.switch(mask - 1, [by(flip) for flip in range(1, size)], parcel)  30.7 us
    ppermute x2, starting transfers between devices, by(): lax.ppermute(block, 'seq', [(i, i ^ flip) for i in range(size)])  21.3 us
  transfers between devices with their start and end apart: 2, of which 2 were waited for; matrix products, arithmetic and copies ran while one was open for 0% of the time, Pallas kernels for 0%

profile of v1, /device:TPU:8, one launch (start us, length us, event | category | flops | bytes accessed | tf_op | source)
XLA Modules:
  0.0 281.7 jit_solution(119545405800756207)
XLA Ops:
  0.6 0.0 copy-start
  0.6 0.0 copy-start.1
  1.3 0.0 copy-done
  1.3 0.6 constant_dynamic-slice_fusion
  2.6 1.1 dynamic-slice_bitcast_fusion
  3.7 0.1 pad_maximum_fusion
  3.7 62.4 %conditional.2 = (bf16[2,128,1024]{2,1,0:T(8,128)(2,1)}) conditional(s32[]{:T(128)} %clamp.4, bf16[2,128,1024]{2,1,0:T(8,128)(2,1)S(1)} %pad_maximum_fusion, bf16[2,128,1024]{2,1,0:T(8,128)(2,1)S(1)} %pad_maximum_fusion, bf16[2,128,1024]{2,1,0:T(8,128)(2,1)S(1)} %pad_maximum_fusion, ...), branch_computations={%region_1.2_spmd, %region_2.3_spmd, %region_3.4_spmd, %region_4.5_... | conditional | bytes 2097200 | solution.py:407
  13.2 12.8 %collective-permute-start.42 = (bf16[2,128,1024]{2,1,0:T(8,128)(2,1)S(1)}, bf16[2,128,1024]{2,1,0:T(8,128)(2,1)}, u32[]{:S(2)}, u32[]{:S(2)}) collective-permute-start(bf16[2,128,1024]{2,1,0:T(8,128)(2,1)S(1)} %param.42), channel_id=1, source_target_pairs={{0,172},{4,168},{8,164},{12,160},{16,188},{20,184},{24,180},{28,17... | collective-permute-start | bytes 1572872 | tf_op jit(solution)/shard_map/cond/branch_42_fun/ppermute | solution.py:405
  26.0 29.8 %collective-permute-done.42 = bf16[2,128,1024]{2,1,0:T(8,128)(2,1)} collective-permute-done((bf16[2,128,1024]{2,1,0:T(8,128)(2,1)S(1)}, bf16[2,128,1024]{2,1,0:T(8,128)(2,1)}, u32[]{:S(2)}, u32[]{:S(2)}) %collective-permute-start.42) | collective-permute-done | bytes 524320 | tf_op jit(solution)/shard_map/cond/branch_42_fun/ppermute | solution.py:405
  66.1 0.0 copy-done.1
  66.1 0.7 broadcast_in_dim_tile.4.pos_ref
  66.8 46.3 %shard_map.102 = (bf16[8,4,32,1024]{3,2,1,0:T(8,128)(2,1)}, bf16[2,128,1024]{2,1,0:T(8,128)(2,1)}, bf16[2,128,1024]{2,1,0:T(8,128)(2,1)}) custom-call(bf16[256,1024]{1,0:T(8,128)(2,1)} %q_ref.3, bf16[256,1024]{1,0:T(8,128)(2,1)} %k_ref.3, bf16[256,1024]{1,0:T(8,128)(2,1)} %v_ref.3, bf16[256,1024]{1,0:T(8,128)(2,1)} %c_ref.3, ...), custom_call_target="tpu_custom_call" | custom-call | tf_op jit(solution)/shard_map/pallas_call | solution.py:434
  113.1 0.6 or_select_fusion.bias_ref
  113.7 0.1 fusion.5
  113.8 0.8 copy.16.keep_ref
  114.6 53.7 %shard_map.103 = (bf16[256,1024]{1,0:T(8,128)(2,1)}, f32[256,1024]{1,0:T(8,128)}, f32[256,1024]{1,0:T(8,128)}, f32[256,1024]{1,0:T(8,128)}, bf16[2,2,128,1024]{3...) custom-call(bf16[256,1024]{1,0:T(8,128)(2,1)} %q_ref.3, ...), custom_call_target="tpu_custom_call" | custom-call | tf_op jit(solution)/shard_map/pallas_call | solution.py:453
  168.3 56.7 %shard_map.104 = (f32[16,1024]{1,0:T(8,128)}, bf16[2,128,1024]{2,1,0:T(8,128)(2,1)}, bf16[2,128,1024]{2,1,0:T(8,128)(2,1)}) custom-call(bf16[8,4,32,1024]{3,2,1,0:T(8,128)(2,1)} %get-tuple-element.278.part_ref, bf16[2,2,128,1024]{3,2,1,0:T(8,128)(2,1)} %get-tuple-element.279.edge_ref), custom_call_target="tpu_custom_call" | custom-call | tf_op jit(solution)/shard_map/pallas_call | solution.py:469
  225.1 49.2 %conditional.3 = (bf16[2,128,1024]{2,1,0:T(8,128)(2,1)}) conditional(s32[]{:T(128)} %clamp.4, bf16[2,128,1024]{2,1,0:T(8,128)(2,1)S(1)} %get-tuple-element.283, bf16[2,128,1024]{2,1,0:T(8,128)(2,1)S(1)} %get-tuple-element.283, bf16[2,128,1024]{2,1,0:T(8,128)(2,1)S(1)} %get-tuple-element.283, ...), branch_computations={%region_64.65_spmd, %region_65.66_spmd, %region_66.67_spmd, %regio... | conditional | bytes 2097200 | solution.py:407
  234.7 8.5 %collective-permute-start.105 = (bf16[2,128,1024]{2,1,0:T(8,128)(2,1)S(1)}, bf16[2,128,1024]{2,1,0:T(8,128)(2,1)}, u32[]{:S(2)}, u32[]{:S(2)}) collective-permute-start(bf16[2,128,1024]{2,1,0:T(8,128)(2,1)S(1)} %param.105), channel_id=1, source_target_pairs={{0,172},{4,168},{8,164},{12,160},{16,188},{20,184},{24,180},{28,17... | collective-permute-start | bytes 1572872 | tf_op jit(solution)/shard_map/cond/branch_42_fun/ppermute | solution.py:405
  243.2 29.8 %collective-permute-done.105 = bf16[2,128,1024]{2,1,0:T(8,128)(2,1)} collective-permute-done((bf16[2,128,1024]{2,1,0:T(8,128)(2,1)S(1)}, bf16[2,128,1024]{2,1,0:T(8,128)(2,1)}, u32[]{:S(2)}, u32[]{:S(2)}) %collective-permute-start.105) | collective-permute-done | bytes 524320 | tf_op jit(solution)/shard_map/cond/branch_42_fun/ppermute | solution.py:405
  274.3 1.3 fusion.4.land_ref
  275.6 0.6 reshape_broadcast_in_dim_tile.3.pos_ref
  276.2 5.2 %shard_map.105 = (bf16[256,1024]{1,0:T(8,128)(2,1)}, bf16[256,1024]{1,0:T(8,128)(2,1)}, bf16[256,1024]{1,0:T(8,128)(2,1)}, bf16[256,1024]{1,0:T(8,128)(2,1)}) custom-call(bf16[256,1024]{1,0:T(8,128)(2,1)} %get-tuple-element.274.out_ref, f32[256,1024]{1,0:T(8,128)} %get-tuple-element.275.dq_ref, f32[256,1024]{1,0:T(8,128)} %get-tuple-element.276.dk_ref, ...), custom_call_target="tpu_custom_call" | custom-call | tf_op jit(solution)/shard_map/pallas_call | solution.py:487
  (3 shorter events, 0.0 us)
Async XLA Ops:
  0.6 0.7 copy-start
  0.6 65.5 %copy-start.1 = (s32[4]{0:T(128)S(1)}, s32[4]{0:T(128)}, u32[]{:S(2)}) copy-start(s32[4]{0:T(128)} %param.137) | copy-start | bytes 52
  13.2 42.6 %collective-permute-start.42 = (bf16[2,128,1024]{2,1,0:T(8,128)(2,1)S(1)}, bf16[2,128,1024]{2,1,0:T(8,128)(2,1)}, u32[]{:S(2)}, u32[]{:S(2)}) collective-permute-start(bf16[2,128,1024]{2,1,0:T(8,128)(2,1)S(1)} %param.42), channel_id=1, source_target_pairs={{0,172},{4,168},{8,164},{12,160},{16,188},{20,184},{24,180},{28,17... | collective-permute-start | bytes 1572872 | tf_op jit(solution)/shard_map/cond/branch_42_fun/ppermute | solution.py:405
  234.7 38.2 %collective-permute-start.105 = (bf16[2,128,1024]{2,1,0:T(8,128)(2,1)S(1)}, bf16[2,128,1024]{2,1,0:T(8,128)(2,1)}, u32[]{:S(2)}, u32[]{:S(2)}) collective-permute-start(bf16[2,128,1024]{2,1,0:T(8,128)(2,1)S(1)} %param.105), channel_id=1, source_target_pairs={{0,172},{4,168},{8,164},{12,160},{16,188},{20,184},{24,180},{28,17... | collective-permute-start | bytes 1572872 | tf_op jit(solution)/shard_map/cond/branch_42_fun/ppermute | solution.py:405
